TPU v7x, 32 devices: a whole 2x2x4 slice. The times are simulated.
32 devices in a mesh: parts: 2 (over y), pencil: 4 (over z), slab: 2 (over x), field: 2 (over core).
Axes of the slice: x: 2, y: 2, z: 4, core: 2. Of those that a mesh axis runs over, the one named last changes fastest.
Arguments:
- state: bfloat16 [16, 2, 512, 512], P('parts', 'slab', 'pencil'), parts along dimension 0, may hold values from -6 to 6
- tangents: bfloat16 [16, 8, 2, 512, 512], P(('parts', 'field'), None, 'slab', 'pencil'), parts along dimension 0, may hold values from -6 to 6
- d1: bfloat16 [512, 512], replicated, may hold values from -0.25 to 0.25
- d2: bfloat16 [512, 512], replicated, may hold values from -0.25 to 0.25
- filt: bfloat16 [512, 512], replicated, may hold values from -0.25 to 0.25
- advect: float32 [2, 8], replicated, may hold values from 0.3 to 1
- diffuse: float32 [8], replicated, may hold values from 0.3 to 1
- coef: float32 [8, 8], replicated, may hold values from -3 to 3
- rates: float32 [8, 8], replicated, may hold values from -3.6 to 3.6
Outputs:
- state_out: bfloat16 [16, 2, 512, 512], P('parts', 'slab', 'pencil'), parts along dimension 0
- tangent_out: bfloat16 [16, 8, 2, 512, 512], P(('parts', 'field'), None, 'slab', 'pencil'), parts along dimension 0
There are 2 independent parts, one for each index of `parts`. A program takes and returns all parts, laid end to end along the dimension named above; an argument that names none is the same for every part. Nothing has to cross between parts.
All inputs are finite; a program needn't handle non-finite values.
Results may differ from a plain program's by a relative error of at most 0.0094.
Values may be sent and summed in bfloat16 or wider, within the bound.
No kernel may reach another device: no remote copies, remote signals or barrier semaphores. Data moves between devices by JAX's collectives and lax.ppermute only.
A program may use at most 128 MiB of HBM per device.

v0:
```python
import jax
import jax.numpy as jnp
from jax import lax
from jax.sharding import PartitionSpec as P

highest = lax.Precision.HIGHEST
time_step = 0.4


def spread(values, fields):
    return values.reshape(values.shape + (1,) * (fields.ndim - values.ndim))


def reaction(state, tangent, coef, rates, offset):
    state_float = state.astype(jnp.float32)
    argument = jnp.einsum("ps,s...->p...", rates, state_float, precision=highest)
    activity = jnp.tanh(argument)
    slopes = 1.0 - activity * activity
    state_rate = jnp.einsum("ps,p...->s...", coef, activity, precision=highest)
    tangent_float = tangent.astype(jnp.float32)
    mixing = jnp.einsum("pt,qt...->qp...", rates, tangent_float, precision=highest)
    number = tangent.shape[0]
    own_coef = lax.dynamic_slice_in_dim(coef, offset, number, 0)
    own_activity = lax.dynamic_slice_in_dim(activity, offset, number, 0)
    tangent_rate = jnp.einsum("ps,qp...->qs...", coef, slopes[None] * mixing, precision=highest)
    tangent_rate = tangent_rate + spread(own_coef, tangent) * own_activity[:, None]
    return (state_rate, tangent_rate)


def update(fields, rate, speeds, diffusivity, operators):
    derivative_op, diffusion_op, filter_op = operators
    slope_term = jnp.dot(fields, derivative_op, preferred_element_type=jnp.float32)
    curve_term = jnp.dot(fields, diffusion_op, preferred_element_type=jnp.float32)
    middle = fields.astype(jnp.float32) + time_step * (
        spread(diffusivity, fields) * curve_term - spread(speeds, fields) * slope_term + rate
    )
    middle = middle.astype(jnp.bfloat16)
    return jnp.dot(middle, filter_op, preferred_element_type=jnp.float32).astype(jnp.bfloat16)


def local(state, tangents, d1, d2, filt, advect, diffuse, coef, rates):
    field_index = lax.axis_index("field")
    params_here = tangents.shape[0]
    state_count = state.shape[0]
    offset = field_index * params_here
    operators = (d1, d2, filt)
    for direction in range(2):
        speeds = advect[direction]
        state_rate, tangent_rate = reaction(state, tangents, coef, rates, offset)
        tangents = update(tangents, tangent_rate, speeds[None, :], diffuse[None, :], operators)
        outgoing = update(state, state_rate, speeds, diffuse, operators)
        merged = tangents.reshape((params_here * state_count,) + tangents.shape[2:])
        arrived, merged = (
            lax.all_to_all(outgoing, "pencil", split_axis=3, concat_axis=2, tiled=True),
            lax.all_to_all(merged, "pencil", split_axis=3, concat_axis=2, tiled=True),
        )
        arrived = jnp.swapaxes(arrived, 2, 3)
        merged = jnp.swapaxes(merged, 2, 3)
        tangents = merged.reshape((params_here, state_count) + merged.shape[1:])
        state = arrived
    return (state, tangents)


def solution(mesh):
    in_specs = (
        P("parts", "slab", "pencil", None),
        P(("parts", "field"), None, "slab", "pencil", None),
        P(),
        P(),
        P(),
        P(),
        P(),
        P(),
        P(),
    )
    out_specs = (
        P("parts", "slab", "pencil", None),
        P(("parts", "field"), None, "slab", "pencil", None),
    )
    return jax.shard_map(local, mesh=mesh, in_specs=in_specs, out_specs=out_specs, check_vma=False)
```

profile of v0, /device:TPU:0, one launch (start us, length us, event | category | flops | bytes accessed | tf_op | source)
XLA Modules:
  0.0 366.4 jit_solution(3940533547604179620)
XLA Ops:
  0.6 0.0 copy-start
  0.6 0.0 copy-start.6
  0.7 0.8 slice_bitcast_fusion
  1.5 0.2 copy-done
  1.7 3.2 fusion.76
  5.0 2.1 multiply_subtract_fusion
  7.1 1.3 copy-done.3
  8.4 3.3 fusion.83
  11.7 6.4 %fusion.54 = bf16[8,1,128,512]{3,2,0,1:T(8,128)(2,1)} fusion(f32[128,512,8]{1,2,0:T(8,128)} %fusion.83, f32[8,128,512]{2,1,0:T(8,128)} %fusion.76, bf16[8,1,128,512]{3,2,1,0:T(8,128)(2,1)} %param.9, f32[8]{0:T(128)S(1)} %get-tuple-element.7, f32[8]{0:T(128)S(1)} %copy-done.10, bf16[512,512]{1,0:T(8,128)(2,1)S(1)} %copy-done.9, bf16[512,512]{1,0:T(8,128)(2,1)} %param.11), kind=kOutput, calls=%fused_computation.58 | convolution fusion | flops 1078460416 | bytes 7340096 | tf_op jit(solution)/shard_map/dot_general | solution.py:38
  18.1 2.4 copy.82
  20.5 6.5 %all-to-all-start = ((bf16[8,1,128,512]{2,0,1,3:T(8,128)(2,1)}), bf16[8,1,128,512]{2,0,1,3:T(8,128)(2,1)}, u32[]{:S(2)}, u32[]{:S(2)}) async-start(bf16[8,1,128,512]{2,0,1,3:T(8,128)(2,1)} %copy.82), calls=%async_computation | async-start | bytes 2097152 | tf_op jit(solution)/shard_map/all_to_all | solution.py:54
  27.1 0.0 copy-start.2
  27.1 2.0 constant_dynamic-slice_fusion
  29.1 1.3 copy.93
  30.4 5.7 %fusion.66 = f32[4,8,128,512]{3,2,1,0:T(8,128)} fusion(bf16[512,512]{1,0:T(8,128)(2,1)S(1)} %copy-done, bf16[4,8,1,128,512]{4,3,2,1,0:T(8,128)(2,1)S(1)} %copy-done.2), kind=kOutput, calls=%fused_computation.70 | convolution fusion | flops 2147483648 | bytes 13107200 | tf_op jit(solution)/shard_map/dot_general | solution.py:33
  36.1 5.6 %fusion.21 = f32[4,128,512,8]{2,3,1,0:T(8,128)S(1)} fusion(bf16[4,8,128,512]{3,2,1,0:T(8,128)(2,1)S(1)} %bitcast.280, f32[8,8]{1,0:T(8,128)S(1)} %copy-done.8), kind=kOutput, calls=%fused_computation.22 | convolution fusion | flops 201326592 | bytes 12583168 | tf_op jit(solution)/shard_map/pt,qt...->qp.../dot_general | solution.py:21
  41.7 10.2 %fusion.12 = f32[4,128,512,8]{2,3,1,0:T(8,128)} fusion(f32[4,128,512,8]{2,3,1,0:T(8,128)S(1)} %fusion.21, f32[8,128,512]{2,0,1:T(8,128)S(1)} %get-tuple-element.8, f32[8,8]{1,0:T(8,128)S(1)} %copy-done.7), kind=kOutput, calls=%fused_computation.15 | convolution fusion | flops 203423744 | bytes 18874624 | tf_op jit(solution)/shard_map/ps,qp...->qs.../dot_general | solution.py:25
  51.9 20.5 %fusion.39 = bf16[4,8,128,512]{3,2,1,0:T(8,128)(2,1)} fusion(f32[4,128,512,8]{2,3,1,0:T(8,128)} %fusion.12, f32[4,8,128,512]{3,2,1,0:T(8,128)} %fusion.66, bf16[4,8,1,128,512]{4,3,2,1,0:T(8,128)(2,1)} %param.10, f32[4,128,512]{2,1,0:T(8,128)} %copy.93, f32[4,8]{1,0:T(4,128)S(1)} %constant_dynamic-slice_fusion.1, f32[8]{0:T(128)S(1)} %get-tuple-element.7, ...), kind=kOutput, calls=%fused_computation.37 | convolution fusion | flops 4318035968 | bytes 27263168 | tf_op jit(solution)/shard_map/dot_general | solution.py:38
  72.3 7.9 %copy.94 = bf16[32,1,128,512]{2,0,1,3:T(8,128)(2,1)} copy(bf16[32,1,128,512]{3,2,0,1:T(8,128)(2,1)} %bitcast.285) | data formatting | bytes 8388608 | tf_op jit(solution)/shard_map/reshape | solution.py:52
  80.3 0.0 all-to-all-done
  80.3 5.4 %all-to-all-start.2 = ((bf16[32,1,128,512]{2,0,1,3:T(8,128)(2,1)}), bf16[32,1,128,512]{2,0,1,3:T(8,128)(2,1)}, u32[]{:S(2)}, u32[]{:S(2)}) async-start(bf16[32,1,128,512]{2,0,1,3:T(8,128)(2,1)} %copy.94), calls=%async_computation.2 | async-start | bytes 8388608 | tf_op jit(solution)/shard_map/all_to_all | solution.py:55
  85.6 2.0 copy.151
  87.7 0.4 all_to_all.55
  88.1 0.0 copy-start.5
  88.1 2.0 fusion.74
  90.2 2.7 fusion.49
  92.9 1.4 copy-done.4
  94.3 3.3 fusion.47
  97.6 6.4 %fusion.55 = bf16[8,1,128,512]{3,2,0,1:T(8,128)(2,1)} fusion(f32[128,512,8]{1,2,0:T(8,128)} %fusion.47, f32[8,128,512]{2,1,0:T(8,128)} %fusion.74, bf16[8,1,512,128]{2,3,0,1:T(8,128)(2,1)} %copy-done.5, f32[8]{0:T(128)S(1)} %get-tuple-element.6, f32[8]{0:T(128)S(1)} %copy-done.10, bf16[512,512]{1,0:T(8,128)(2,1)S(1)} %copy-done.9, bf16[512,512]{1,0:T(8,128)(2,1)} %param.11), kind=kOutput, calls=%fused_computation.59 | convolution fusion | flops 1078460416 | bytes 7340096 | tf_op jit(solution)/shard_map/dot_general | solution.py:38
  104.0 2.4 copy.87
  106.4 1.8 dynamic-slice_bitcast_fusion
  108.3 1.3 copy.99
  109.6 69.0 %all-to-all-done.2 = bf16[32,1,128,512]{2,0,1,3:T(8,128)(2,1)} async-done(((bf16[32,1,128,512]{2,0,1,3:T(8,128)(2,1)}), bf16[32,1,128,512]{2,0,1,3:T(8,128)(2,1)}, u32[]{:S(2)}, u32[]{:S(2)}) %all-to-all-start.2) | async-done | bytes 4194336 | tf_op jit(solution)/shard_map/all_to_all | solution.py:55
  178.6 4.7 %all-to-all-start.1 = ((bf16[8,1,128,512]{2,0,1,3:T(8,128)(2,1)}), bf16[8,1,128,512]{2,0,1,3:T(8,128)(2,1)}, u32[]{:S(2)}, u32[]{:S(2)}) async-start(bf16[8,1,128,512]{2,0,1,3:T(8,128)(2,1)} %copy.87), calls=%async_computation.1 | async-start | bytes 2097152 | tf_op jit(solution)/shard_map/all_to_all | solution.py:54
  183.3 7.4 %copy.95 = bf16[32,1,4,128,128]{3,2,4,0,1:T(4,128)(2,1)} copy(bf16[32,1,4,128,128]{3,0,4,2,1:T(8,128)(2,1)} %bitcast.47) | data formatting | bytes 8388608 | tf_op jit(solution)/shard_map/all_to_all | solution.py:55
  190.7 7.2 %all_to_all.63 = bf16[32,1,512,128]{2,3,0,1:T(8,128)(2,1)} reshape(bf16[32,1,4,128,128]{3,2,4,0,1:T(4,128)(2,1)} %copy.95) | data formatting | bytes 8388608 | tf_op jit(solution)/shard_map/all_to_all | solution.py:55
  197.9 8.0 %fusion.19 = f32[4,128,512,8]{2,3,1,0:T(8,128)S(1)} fusion(bf16[4,8,128,512]{3,2,1,0:T(8,128)(2,1)} %bitcast.276, f32[8,8]{1,0:T(8,128)S(1)} %copy-done.8), kind=kOutput, calls=%fused_computation.20 | convolution fusion | flops 201326592 | bytes 12583168 | tf_op jit(solution)/shard_map/pt,qt...->qp.../dot_general | solution.py:21
  205.9 5.6 %fusion.64 = f32[4,8,128,512]{3,2,1,0:T(8,128)} fusion(bf16[4,8,128,512]{3,2,1,0:T(8,128)(2,1)S(1)} %bitcast.279, bf16[512,512]{1,0:T(8,128)(2,1)S(1)} %copy-done), kind=kOutput, calls=%fused_computation.68 | convolution fusion | flops 2147483648 | bytes 13107200 | tf_op jit(solution)/shard_map/dot_general | solution.py:33
  211.5 10.1 %fusion.5 = f32[4,128,512,8]{2,3,1,0:T(8,128)} fusion(f32[4,128,512,8]{2,3,1,0:T(8,128)S(1)} %fusion.19, f32[8,128,512]{2,0,1:T(8,128)S(1)} %get-tuple-element.10, f32[8,8]{1,0:T(8,128)S(1)} %copy-done.7), kind=kOutput, calls=%fused_computation.7 | convolution fusion | flops 203423744 | bytes 18874624 | tf_op jit(solution)/shard_map/ps,qp...->qs.../dot_general | solution.py:25
  221.6 20.4 %fusion.42 = bf16[4,8,128,512]{3,2,1,0:T(8,128)(2,1)} fusion(f32[4,128,512]{2,1,0:T(8,128)} %copy.99, f32[4,128,512,8]{2,3,1,0:T(8,128)} %fusion.5, f32[4,8,128,512]{3,2,1,0:T(8,128)} %fusion.64, bf16[4,8,1,128,512]{4,3,1,0,2:T(8,128)(2,1)} %bitcast.278, f32[8]{0:T(128)S(1)} %get-tuple-element.6, f32[4,8]{1,0:T(4,128)S(1)} %constant_dynamic-slice_fusion.1, ...), kind=kOutput, calls=%fused_computation.38 | convolution fusion | flops 4318035968 | bytes 31457472 | tf_op jit(solution)/shard_map/dot_general | solution.py:38
  242.0 7.9 %copy.100 = bf16[32,1,128,512]{2,0,1,3:T(8,128)(2,1)} copy(bf16[32,1,128,512]{3,2,0,1:T(8,128)(2,1)} %bitcast.284) | data formatting | bytes 8388608 | tf_op jit(solution)/shard_map/reshape | solution.py:52
  249.9 5.3 %all-to-all-start.3 = ((bf16[32,1,128,512]{2,0,1,3:T(8,128)(2,1)}), bf16[32,1,128,512]{2,0,1,3:T(8,128)(2,1)}, u32[]{:S(2)}, u32[]{:S(2)}) async-start(bf16[32,1,128,512]{2,0,1,3:T(8,128)(2,1)} %copy.100), calls=%async_computation.3 | async-start | bytes 8388608 | tf_op jit(solution)/shard_map/all_to_all | solution.py:55
  255.2 2.0 copy.88
  257.2 1.2 all_to_all.59
  258.4 89.3 %all-to-all-done.3 = bf16[32,1,128,512]{2,0,1,3:T(8,128)(2,1)} async-done(((bf16[32,1,128,512]{2,0,1,3:T(8,128)(2,1)}), bf16[32,1,128,512]{2,0,1,3:T(8,128)(2,1)}, u32[]{:S(2)}, u32[]{:S(2)}) %all-to-all-start.3) | async-done | bytes 4194336 | tf_op jit(solution)/shard_map/all_to_all | solution.py:55
  347.7 5.8 %copy.101 = bf16[32,1,128,512]{2,3,0,1:T(8,128)(2,1)} copy(bf16[32,1,128,512]{2,0,1,3:T(8,128)(2,1)} %all-to-all-done.3) | data formatting | bytes 8388608 | tf_op jit(solution)/shard_map/all_to_all | solution.py:55
  353.6 6.5 %copy.102 = bf16[32,1,4,128,128]{4,3,2,0,1:T(8,128)(2,1)} copy(bf16[32,1,4,128,128]{3,4,2,0,1:T(8,128)(2,1)} %bitcast.281) | data formatting | bytes 8388608 | tf_op jit(solution)/shard_map/all_to_all | solution.py:55
  360.0 6.2 %copy.103 = bf16[4,8,1,128,512]{4,3,2,1,0:T(8,128)(2,1)} copy(bf16[4,8,1,128,512]{3,4,1,0,2:T(8,128)(2,1)} %bitcast.282) | data formatting | bytes 8388608
  (17 shorter events, 0.0 us)
Async XLA Ops:
  0.6 1.1 copy-start
  0.6 4.3 %copy-start.6 = (bf16[8,1,128,512]{3,2,1,0:T(8,128)(2,1)S(1)}, bf16[8,1,128,512]{3,2,1,0:T(8,128)(2,1)}, u32[]{:S(2)}) copy-start(bf16[8,1,128,512]{3,2,1,0:T(8,128)(2,1)} %param.9) | copy-start | bytes 3145732
  1.7 6.7 %copy-start.7 = (f32[8,8]{1,0:T(8,128)S(1)}, f32[8,8]{1,0:T(8,128)}, u32[]{:S(2)}) copy-start(f32[8,8]{1,0:T(8,128)} %param.16) | copy-start | bytes 772
  5.0 6.7 %copy-start.9 = (bf16[512,512]{1,0:T(8,128)(2,1)S(1)}, bf16[512,512]{1,0:T(8,128)(2,1)}, u32[]{:S(2)}) copy-start(bf16[512,512]{1,0:T(8,128)(2,1)} %param.13) | copy-start | bytes 1572868
  5.0 6.7 %copy-start.10 = (f32[8]{0:T(128)S(1)}, f32[8]{0:T(128)}, u32[]{:S(2)}) copy-start(f32[8]{0:T(128)} %param.15) | copy-start | bytes 100
  7.1 1.3 copy-start.3
  20.5 59.7 %all-to-all-start = ((bf16[8,1,128,512]{2,0,1,3:T(8,128)(2,1)}), bf16[8,1,128,512]{2,0,1,3:T(8,128)(2,1)}, u32[]{:S(2)}, u32[]{:S(2)}) async-start(bf16[8,1,128,512]{2,0,1,3:T(8,128)(2,1)} %copy.82), calls=%async_computation | async-start | bytes 2097152 | tf_op jit(solution)/shard_map/all_to_all | solution.py:54
  27.1 3.3 copy-start.2
  30.4 5.7 %copy-start.8 = (f32[8,8]{1,0:T(8,128)S(1)}, f32[8,8]{1,0:T(8,128)}, u32[]{:S(2)}) copy-start(f32[8,8]{1,0:T(8,128)} %param.17) | copy-start | bytes 772
  80.3 98.3 %all-to-all-start.2 = ((bf16[32,1,128,512]{2,0,1,3:T(8,128)(2,1)}), bf16[32,1,128,512]{2,0,1,3:T(8,128)(2,1)}, u32[]{:S(2)}, u32[]{:S(2)}) async-start(bf16[32,1,128,512]{2,0,1,3:T(8,128)(2,1)} %copy.94), calls=%async_computation.2 | async-start | bytes 8388608 | tf_op jit(solution)/shard_map/all_to_all | solution.py:55
  88.1 2.0 copy-start.5
  92.9 1.4 copy-start.4
  178.6 71.3 %all-to-all-start.1 = ((bf16[8,1,128,512]{2,0,1,3:T(8,128)(2,1)}), bf16[8,1,128,512]{2,0,1,3:T(8,128)(2,1)}, u32[]{:S(2)}, u32[]{:S(2)}) async-start(bf16[8,1,128,512]{2,0,1,3:T(8,128)(2,1)} %copy.87), calls=%async_computation.1 | async-start | bytes 2097152 | tf_op jit(solution)/shard_map/all_to_all | solution.py:54
  197.9 8.0 %copy-start.1 = (bf16[32,1,512,128]{2,3,0,1:T(8,128)(2,1)S(1)}, bf16[32,1,512,128]{2,3,0,1:T(8,128)(2,1)}, u32[]{:S(2)}) copy-start(bf16[32,1,512,128]{2,3,0,1:T(8,128)(2,1)} %all_to_all.63) | copy-start | bytes 12582916
  249.9 97.8 %all-to-all-start.3 = ((bf16[32,1,128,512]{2,0,1,3:T(8,128)(2,1)}), bf16[32,1,128,512]{2,0,1,3:T(8,128)(2,1)}, u32[]{:S(2)}, u32[]{:S(2)}) async-start(bf16[32,1,128,512]{2,0,1,3:T(8,128)(2,1)} %copy.100), calls=%async_computation.3 | async-start | bytes 8388608 | tf_op jit(solution)/shard_map/all_to_all | solution.py:55
where the time goes:
time: 373 us; the launch traced here: 366 us
  waiting for transfers between devices  158 us (42%)
  matrix products  115 us (31%)
  local copies, waits for them, and re-layouts  69.8 us (19%)
  starting transfers between devices  21.9 us (6%)
    all_to_all x2, waiting for transfers between devices, local(): lax.all_to_all(merged, 'pencil', split_axis=3, concat_axis=2, tiled=True)  158 us
    dot_general x4, matrix products, update(): jnp.dot(middle, filter_op, preferred_element_type=jnp.float32)  53.6 us
    all_to_all x4, local copies, waits for them, and re-layouts, local(): lax.all_to_all(merged, 'pencil', split_axis=3, concat_axis=2, tiled=True)  26.9 us
    dot_general x2, matrix products, reaction(): jnp.einsum('ps,qp...->qs...', coef, slopes[None] * mixing, precision=high...  20.3 us
    dot_general x4, matrix products, update(): jnp.dot(fields, diffusion_op, preferred_element_type=jnp.float32)  16.5 us
    reshape x2, local copies, waits for them, and re-layouts, local(): merged = tangents.reshape((params_here * state_count,) + tangents.shape[2:])  15.8 us
    dot_general x2, matrix products, reaction(): jnp.einsum('pt,qt...->qp...', rates, tangent_float, precision=highest)  13.6 us
    all_to_all x2, starting transfers between devices, local(): lax.all_to_all(outgoing, 'pencil', split_axis=3, concat_axis=2, tiled=True)  11.2 us
  transfers between devices with their start and end apart: 4, of which 2 were waited for; matrix products, arithmetic and copies ran while one was open for 37% of the time, Pallas kernels for 0%

commit v1 on v0

--- a/solution.py
+++ b/solution.py
@@ -52,7 +52,12 @@
         merged = tangents.reshape((params_here * state_count,) + tangents.shape[2:])
         arrived, merged = (
             lax.all_to_all(outgoing, "pencil", split_axis=3, concat_axis=2, tiled=True),
-            lax.all_to_all(merged, "pencil", split_axis=3, concat_axis=2, tiled=True),
+            jnp.concatenate(
+                lax.all_to_all(
+                    jnp.stack(jnp.split(merged, lax.axis_size("pencil"), axis=3)), "pencil", 0, 0
+                ),
+                axis=2,
+            ),
         )
         arrived = jnp.swapaxes(arrived, 2, 3)
         merged = jnp.swapaxes(merged, 2, 3)

time: 373 us -> 360 us (0.965)
  local copies, waits for them, and re-layouts: 69.8 us -> 52 us
  other arithmetic: 0 us -> 4.59 us
    all_to_all x4 -> x1, local copies, waits for them, and re-layouts: 26.9 us -> 4.78 us  [local(): lax.all_to_all(jnp.stack(jnp.split(merged, lax.axis_size('pencil'), axis=...]
    another operation x4 -> x6, local copies, waits for them, and re-layouts: 6.44 us -> 12 us
    another operation x0 -> x2, other arithmetic: none -> 4.59 us  [local(): jnp.stack(jnp.split(merged, lax.axis_size('pencil'), axis=3))]
  transfers between devices with their start and end apart: 4 -> 4, of which waited for: 2 -> 2; matrix products, arithmetic and copies ran while one was open for 37% -> 39% of each run, Pallas kernels for 0% -> 0%
where the time goes in v1:
time: 360 us; the launch traced here: 354 us
  waiting for transfers between devices  158 us (44%)
  matrix products  116 us (32%)
  local copies, waits for them, and re-layouts  52 us (14%)
  starting transfers between devices  21.8 us (6%)
  other arithmetic  4.59 us (1%)
    all_to_all x2, waiting for transfers between devices, local(): lax.all_to_all(jnp.stack(jnp.split(merged, lax.axis_size('pencil'), axis=...  158 us
    dot_general x4, matrix products, update(): jnp.dot(middle, filter_op, preferred_element_type=jnp.float32)  54 us
    dot_general x2, matrix products, reaction(): jnp.einsum('ps,qp...->qs...', coef, slopes[None] * mixing, precision=high...  20.1 us
    dot_general x4, matrix products, update(): jnp.dot(fields, diffusion_op, preferred_element_type=jnp.float32)  16.5 us
    reshape x2, local copies, waits for them, and re-layouts, local(): jnp.concatenate(lax.all_to_all(jnp.stack(jnp.split(merged, lax.axis_size(...  14.6 us
    dot_general x2, matrix products, reaction(): jnp.einsum('pt,qt...->qp...', rates, tangent_float, precision=highest)  13.6 us
    all_to_all x2, starting transfers between devices, local(): lax.all_to_all(outgoing, 'pencil', split_axis=3, concat_axis=2, tiled=True)  11.4 us
    all_to_all x2, starting transfers between devices, local(): lax.all_to_all(jnp.stack(jnp.split(merged, lax.axis_size('pencil'), axis=...  10.4 us
  transfers between devices with their start and end apart: 4, of which 2 were waited for; matrix products, arithmetic and copies ran while one was open for 39% of the time, Pallas kernels for 0%

profile of v1, /device:TPU:0, one launch (start us, length us, event | category | flops | bytes accessed | tf_op | source)
XLA Modules:
  0.0 353.7 jit_solution(4262573621626134658)
XLA Ops:
  0.6 0.0 copy-start
  0.6 0.0 copy-start.6
  0.7 0.8 slice_bitcast_fusion.8
  1.5 0.2 copy-done
  1.7 3.2 fusion.76
  5.0 2.1 multiply_subtract_fusion
  7.1 1.3 copy-done.3
  8.4 3.3 fusion.83
  11.7 6.4 %fusion.54 = bf16[8,1,128,512]{3,2,0,1:T(8,128)(2,1)} fusion(f32[128,512,8]{1,2,0:T(8,128)} %fusion.83, f32[8,128,512]{2,1,0:T(8,128)} %fusion.76, bf16[8,1,128,512]{3,2,1,0:T(8,128)(2,1)} %param.9, f32[8]{0:T(128)S(1)} %get-tuple-element.15, f32[8]{0:T(128)S(1)} %copy-done.10, bf16[512,512]{1,0:T(8,128)(2,1)S(1)} %copy-done.9, bf16[512,512]{1,0:T(8,128)(2,1)} %param.11), kind=kOutput, calls=%fused_computation.60 | convolution fusion | flops 1078460416 | bytes 7340096 | tf_op jit(solution)/shard_map/dot_general | solution.py:38
  18.1 2.4 copy.57
  20.5 6.9 %all-to-all-start = ((bf16[8,1,128,512]{2,0,1,3:T(8,128)(2,1)}), bf16[8,1,128,512]{2,0,1,3:T(8,128)(2,1)}, u32[]{:S(2)}, u32[]{:S(2)}) async-start(bf16[8,1,128,512]{2,0,1,3:T(8,128)(2,1)} %copy.57), calls=%async_computation | async-start | bytes 2097152 | tf_op jit(solution)/shard_map/all_to_all | solution.py:54
  27.4 0.0 copy-start.2
  27.4 2.0 constant_dynamic-slice_fusion
  29.4 1.3 copy.68
  30.7 5.7 %fusion.66 = f32[4,8,128,512]{3,2,1,0:T(8,128)} fusion(bf16[512,512]{1,0:T(8,128)(2,1)S(1)} %copy-done, bf16[4,8,1,128,512]{4,3,2,1,0:T(8,128)(2,1)S(1)} %copy-done.2), kind=kOutput, calls=%fused_computation.80 | convolution fusion | flops 2147483648 | bytes 13107200 | tf_op jit(solution)/shard_map/dot_general | solution.py:33
  36.4 5.6 %fusion.21 = f32[4,128,512,8]{2,3,1,0:T(8,128)S(1)} fusion(bf16[4,8,128,512]{3,2,1,0:T(8,128)(2,1)S(1)} %bitcast.293, f32[8,8]{1,0:T(8,128)S(1)} %copy-done.8), kind=kOutput, calls=%fused_computation.24 | convolution fusion | flops 201326592 | bytes 12583168 | tf_op jit(solution)/shard_map/pt,qt...->qp.../dot_general | solution.py:21
  42.0 10.2 %fusion.12 = f32[4,128,512,8]{2,3,1,0:T(8,128)} fusion(f32[4,128,512,8]{2,3,1,0:T(8,128)S(1)} %fusion.21, f32[8,128,512]{2,0,1:T(8,128)S(1)} %get-tuple-element.16, f32[8,8]{1,0:T(8,128)S(1)} %copy-done.7), kind=kOutput, calls=%fused_computation.15 | convolution fusion | flops 203423744 | bytes 18874624 | tf_op jit(solution)/shard_map/ps,qp...->qs.../dot_general | solution.py:25
  52.2 20.5 %fusion.39 = bf16[4,8,128,512]{3,2,1,0:T(8,128)(2,1)} fusion(f32[4,128,512,8]{2,3,1,0:T(8,128)} %fusion.12, f32[4,8,128,512]{3,2,1,0:T(8,128)} %fusion.66, bf16[4,8,1,128,512]{4,3,2,1,0:T(8,128)(2,1)} %param.10, f32[4,128,512]{2,1,0:T(8,128)} %copy.68, f32[4,8]{1,0:T(4,128)S(1)} %constant_dynamic-slice_fusion.1, f32[8]{0:T(128)S(1)} %get-tuple-element.15, ...), kind=kOutput, calls=%fused_computation.39 | convolution fusion | flops 4318035968 | bytes 27263168 | tf_op jit(solution)/shard_map/dot_general | solution.py:38
  72.6 2.8 slice_bitcast_fusion.7
  75.4 2.3 pad_maximum_fusion
  77.7 5.3 %all-to-all-start.2 = ((bf16[4,32,1,128,128]{4,3,1,2,0:T(8,128)(2,1)}), bf16[4,32,1,128,128]{4,3,1,2,0:T(8,128)(2,1)}, u32[]{:S(2)}, u32[]{:S(2)}) async-start(bf16[4,32,1,128,128]{4,3,1,2,0:T(8,128)(2,1)} %pad_maximum_fusion), calls=%async_computation.2 | async-start | bytes 8388608 | tf_op jit(solution)/shard_map/all_to_all | solution.py:56
  83.0 2.0 copy.123
  85.1 0.4 all_to_all.35
  85.5 0.0 copy-start.5
  85.5 2.1 fusion.74
  87.6 2.7 fusion.49
  90.4 1.3 copy-done.4
  91.7 3.3 fusion.47
  95.0 6.4 %fusion.55 = bf16[8,1,128,512]{3,2,0,1:T(8,128)(2,1)} fusion(f32[128,512,8]{1,2,0:T(8,128)} %fusion.47, f32[8,128,512]{2,1,0:T(8,128)} %fusion.74, bf16[8,1,512,128]{2,3,0,1:T(8,128)(2,1)} %copy-done.5, f32[8]{0:T(128)S(1)} %get-tuple-element.14, f32[8]{0:T(128)S(1)} %copy-done.10, bf16[512,512]{1,0:T(8,128)(2,1)S(1)} %copy-done.9, bf16[512,512]{1,0:T(8,128)(2,1)} %param.11), kind=kOutput, calls=%fused_computation.61 | convolution fusion | flops 1078460416 | bytes 7340096 | tf_op jit(solution)/shard_map/dot_general | solution.py:38
  101.4 2.4 copy.62
  103.9 1.8 dynamic-slice_bitcast_fusion
  105.7 1.3 copy.73
  107.0 69.0 %all-to-all-done.2 = bf16[4,32,1,128,128]{4,3,1,2,0:T(8,128)(2,1)} async-done(((bf16[4,32,1,128,128]{4,3,1,2,0:T(8,128)(2,1)}), bf16[4,32,1,128,128]{4,3,1,2,0:T(8,128)(2,1)}, u32[]{:S(2)}, u32[]{:S(2)}) %all-to-all-start.2) | async-done | bytes 4194336 | tf_op jit(solution)/shard_map/all_to_all | solution.py:56
  176.0 4.5 %all-to-all-start.1 = ((bf16[8,1,128,512]{2,0,1,3:T(8,128)(2,1)}), bf16[8,1,128,512]{2,0,1,3:T(8,128)(2,1)}, u32[]{:S(2)}, u32[]{:S(2)}) async-start(bf16[8,1,128,512]{2,0,1,3:T(8,128)(2,1)} %copy.62), calls=%async_computation.1 | async-start | bytes 2097152 | tf_op jit(solution)/shard_map/all_to_all | solution.py:54
  180.5 7.4 %copy.69 = bf16[32,1,4,128,128]{3,2,4,0,1:T(4,128)(2,1)} copy(bf16[32,1,4,128,128]{4,3,0,1,2:T(8,128)(2,1)} %bitcast.50) | data formatting | bytes 8388608 | tf_op jit(solution)/shard_map/reshape | solution.py:55
  188.0 7.2 %reshape.193 = bf16[32,1,512,128]{2,3,0,1:T(8,128)(2,1)} reshape(bf16[32,1,4,128,128]{3,2,4,0,1:T(4,128)(2,1)} %copy.69) | data formatting | bytes 8388608 | tf_op jit(solution)/shard_map/reshape | solution.py:55
  195.1 8.0 %fusion.19 = f32[4,128,512,8]{2,3,1,0:T(8,128)S(1)} fusion(bf16[4,8,128,512]{3,2,1,0:T(8,128)(2,1)} %bitcast.289, f32[8,8]{1,0:T(8,128)S(1)} %copy-done.8), kind=kOutput, calls=%fused_computation.22 | convolution fusion | flops 201326592 | bytes 12583168 | tf_op jit(solution)/shard_map/pt,qt...->qp.../dot_general | solution.py:21
  203.2 5.6 %fusion.64 = f32[4,8,128,512]{3,2,1,0:T(8,128)} fusion(bf16[4,8,128,512]{3,2,1,0:T(8,128)(2,1)S(1)} %bitcast.292, bf16[512,512]{1,0:T(8,128)(2,1)S(1)} %copy-done), kind=kOutput, calls=%fused_computation.78 | convolution fusion | flops 2147483648 | bytes 13107200 | tf_op jit(solution)/shard_map/dot_general | solution.py:33
  208.7 10.0 %fusion.5 = f32[4,128,512,8]{2,3,1,0:T(8,128)} fusion(f32[4,128,512,8]{2,3,1,0:T(8,128)S(1)} %fusion.19, f32[8,128,512]{2,0,1:T(8,128)S(1)} %get-tuple-element.18, f32[8,8]{1,0:T(8,128)S(1)} %copy-done.7), kind=kOutput, calls=%fused_computation.7 | convolution fusion | flops 203423744 | bytes 18874624 | tf_op jit(solution)/shard_map/ps,qp...->qs.../dot_general | solution.py:25
  218.7 20.8 %fusion.42 = bf16[4,8,128,512]{3,2,1,0:T(8,128)(2,1)} fusion(f32[4,128,512]{2,1,0:T(8,128)} %copy.73, f32[4,128,512,8]{2,3,1,0:T(8,128)} %fusion.5, f32[4,8,128,512]{3,2,1,0:T(8,128)} %fusion.64, bf16[4,8,1,128,512]{4,3,1,0,2:T(8,128)(2,1)} %bitcast.291, f32[8]{0:T(128)S(1)} %get-tuple-element.14, f32[4,8]{1,0:T(4,128)S(1)} %constant_dynamic-slice_fusion.1, ...), kind=kOutput, calls=%fused_computation.40 | convolution fusion | flops 4318035968 | bytes 31457472 | tf_op jit(solution)/shard_map/dot_general | solution.py:38
  239.5 2.8 slice_bitcast_fusion.3
  242.3 2.3 pad_maximum_fusion.1
  244.6 5.1 %all-to-all-start.3 = ((bf16[4,32,1,128,128]{4,3,1,2,0:T(8,128)(2,1)}), bf16[4,32,1,128,128]{4,3,1,2,0:T(8,128)(2,1)}, u32[]{:S(2)}, u32[]{:S(2)}) async-start(bf16[4,32,1,128,128]{4,3,1,2,0:T(8,128)(2,1)} %pad_maximum_fusion.1), calls=%async_computation.3 | async-start | bytes 8388608 | tf_op jit(solution)/shard_map/all_to_all | solution.py:56
  249.6 2.0 copy.63
  251.7 1.2 all_to_all.39
  252.9 89.3 %all-to-all-done.3 = bf16[4,32,1,128,128]{4,3,1,2,0:T(8,128)(2,1)} async-done(((bf16[4,32,1,128,128]{4,3,1,2,0:T(8,128)(2,1)}), bf16[4,32,1,128,128]{4,3,1,2,0:T(8,128)(2,1)}, u32[]{:S(2)}, u32[]{:S(2)}) %all-to-all-start.3) | async-done | bytes 4194336 | tf_op jit(solution)/shard_map/all_to_all | solution.py:56
  342.2 4.8 %copy.74 = bf16[4,32,1,128,128]{4,3,0,1,2:T(8,128)(2,1)} copy(bf16[4,32,1,128,128]{4,3,1,2,0:T(8,128)(2,1)} %all-to-all-done.3) | data formatting | bytes 8388608 | tf_op jit(solution)/shard_map/all_to_all | solution.py:56
  347.0 6.2 %copy.75 = bf16[4,8,1,128,512]{4,3,2,1,0:T(8,128)(2,1)} copy(bf16[4,8,1,128,512]{3,4,1,0,2:T(8,128)(2,1)} %bitcast.294) | data formatting | bytes 8388608
  (18 shorter events, 0.0 us)
Async XLA Ops:
  0.6 1.1 copy-start
  0.6 4.3 %copy-start.6 = (bf16[8,1,128,512]{3,2,1,0:T(8,128)(2,1)S(1)}, bf16[8,1,128,512]{3,2,1,0:T(8,128)(2,1)}, u32[]{:S(2)}) copy-start(bf16[8,1,128,512]{3,2,1,0:T(8,128)(2,1)} %param.9) | copy-start | bytes 3145732
  1.7 6.7 %copy-start.7 = (f32[8,8]{1,0:T(8,128)S(1)}, f32[8,8]{1,0:T(8,128)}, u32[]{:S(2)}) copy-start(f32[8,8]{1,0:T(8,128)} %param.16) | copy-start | bytes 772
  4.9 6.7 %copy-start.9 = (bf16[512,512]{1,0:T(8,128)(2,1)S(1)}, bf16[512,512]{1,0:T(8,128)(2,1)}, u32[]{:S(2)}) copy-start(bf16[512,512]{1,0:T(8,128)(2,1)} %param.13) | copy-start | bytes 1572868
  5.0 6.7 %copy-start.10 = (f32[8]{0:T(128)S(1)}, f32[8]{0:T(128)}, u32[]{:S(2)}) copy-start(f32[8]{0:T(128)} %param.15) | copy-start | bytes 100
  7.1 1.3 copy-start.3
  20.5 57.2 %all-to-all-start = ((bf16[8,1,128,512]{2,0,1,3:T(8,128)(2,1)}), bf16[8,1,128,512]{2,0,1,3:T(8,128)(2,1)}, u32[]{:S(2)}, u32[]{:S(2)}) async-start(bf16[8,1,128,512]{2,0,1,3:T(8,128)(2,1)} %copy.57), calls=%async_computation | async-start | bytes 2097152 | tf_op jit(solution)/shard_map/all_to_all | solution.py:54
  27.4 3.3 copy-start.2
  30.7 5.7 %copy-start.8 = (f32[8,8]{1,0:T(8,128)S(1)}, f32[8,8]{1,0:T(8,128)}, u32[]{:S(2)}) copy-start(f32[8,8]{1,0:T(8,128)} %param.17) | copy-start | bytes 772
  77.7 98.3 %all-to-all-start.2 = ((bf16[4,32,1,128,128]{4,3,1,2,0:T(8,128)(2,1)}), bf16[4,32,1,128,128]{4,3,1,2,0:T(8,128)(2,1)}, u32[]{:S(2)}, u32[]{:S(2)}) async-start(bf16[4,32,1,128,128]{4,3,1,2,0:T(8,128)(2,1)} %pad_maximum_fusion), calls=%async_computation.2 | async-start | bytes 8388608 | tf_op jit(solution)/shard_map/all_to_all | solution.py:56
  85.5 2.1 copy-start.5
  90.4 1.3 copy-start.4
  176.0 68.6 %all-to-all-start.1 = ((bf16[8,1,128,512]{2,0,1,3:T(8,128)(2,1)}), bf16[8,1,128,512]{2,0,1,3:T(8,128)(2,1)}, u32[]{:S(2)}, u32[]{:S(2)}) async-start(bf16[8,1,128,512]{2,0,1,3:T(8,128)(2,1)} %copy.62), calls=%async_computation.1 | async-start | bytes 2097152 | tf_op jit(solution)/shard_map/all_to_all | solution.py:54
  195.1 8.0 %copy-start.1 = (bf16[32,1,512,128]{2,3,0,1:T(8,128)(2,1)S(1)}, bf16[32,1,512,128]{2,3,0,1:T(8,128)(2,1)}, u32[]{:S(2)}) copy-start(bf16[32,1,512,128]{2,3,0,1:T(8,128)(2,1)} %reshape.193) | copy-start | bytes 12582916
  244.6 97.7 %all-to-all-start.3 = ((bf16[4,32,1,128,128]{4,3,1,2,0:T(8,128)(2,1)}), bf16[4,32,1,128,128]{4,3,1,2,0:T(8,128)(2,1)}, u32[]{:S(2)}, u32[]{:S(2)}) async-start(bf16[4,32,1,128,128]{4,3,1,2,0:T(8,128)(2,1)} %pad_maximum_fusion.1), calls=%async_computation.3 | async-start | bytes 8388608 | tf_op jit(solution)/shard_map/all_to_all | solution.py:56
